TPU v7x, 32 devices: a whole 2x2x4 slice. The times are simulated.
32 devices in a mesh: shard: 2 (over x), ctx: 2 (over core), tensor: 8 (over z, y).
Axes of the slice: x: 2, y: 2, z: 4, core: 2. Of those that a mesh axis runs over, the one named last changes fastest.
Arguments:
- inputs: bfloat16 [2, 1024, 1152], P('shard', 'ctx'), may hold values from -6 to 6
- cotangent: bfloat16 [2, 1024, 1152], P('shard', 'ctx'), may hold values from -6 to 6
- attn_norm_gain: float32 [1152], replicated, may hold values from 0.1 to 1.9
- attn_norm_bias: float32 [1152], replicated, may hold values from -0.1875 to 0.1875
- qkv_weight: bfloat16 [3, 1152, 1152], P(None, 'shard', 'tensor'), may hold values from -0.8249579 to 0.8249579
- query_value_bias: float32 [2, 1152], P(None, 'tensor'), may hold values from -1.8 to 1.8
- out_weight: bfloat16 [1152, 1152], P('tensor', 'shard'), may hold values from -4 to 4
- out_bias: float32 [1152], replicated, may hold values from -1.75 to 1.75
- mlp_norm_gain: float32 [1152], replicated, may hold values from 0.1 to 1.9
- mlp_norm_bias: float32 [1152], replicated, may hold values from -1.75 to 1.75
- up_weight: bfloat16 [1152, 4304], P('shard', 'tensor'), may hold values from -0.1875 to 0.1875
- up_bias: float32 [4304], P('tensor'), may hold values from -1.75 to 1.75
- down_weight: bfloat16 [4304, 1152], P('tensor', 'shard'), may hold values from -0.1875 to 0.1875
- down_bias: float32 [1152], replicated, may hold values from -1.75 to 1.75
Outputs:
- output: bfloat16 [2, 1024, 1152], P('shard', 'ctx')
- inputs_grad: float32 [2, 1024, 1152], P('shard', 'ctx')
- attn_norm_gain_grad: float32 [1152], replicated
- attn_norm_bias_grad: float32 [1152], replicated
- qkv_weight_grad: float32 [3, 1152, 1152], P(None, 'shard', 'tensor')
- query_value_bias_grad: float32 [2, 1152], P(None, 'tensor')
- out_weight_grad: float32 [1152, 1152], P('tensor', 'shard')
- out_bias_grad: float32 [1152], replicated
- mlp_norm_gain_grad: float32 [1152], replicated
- mlp_norm_bias_grad: float32 [1152], replicated
- up_weight_grad: float32 [1152, 4304], P('shard', 'tensor')
- up_bias_grad: float32 [4304], P('tensor')
- down_weight_grad: float32 [4304, 1152], P('tensor', 'shard')
- down_bias_grad: float32 [1152], replicated
All inputs are finite; a program needn't handle non-finite values.
Results may differ from a plain program's by a relative error of at most 0.023.
Values may be sent and summed in bfloat16 or wider, within the bound.
No kernel may reach another device: no remote copies, remote signals or barrier semaphores. Data moves between devices by JAX's collectives and lax.ppermute only.
A program may use at most 128 MiB of HBM per device.

v0:
```python
import jax
import jax.numpy as jnp
from jax import lax
from jax.sharding import PartitionSpec as P

HD = 72
EPSILON = 1e-06


def layer_norm(rows, gain, shift):
    center = jnp.mean(rows, axis=-1, keepdims=True)
    offset = rows - center
    spread = jnp.mean(offset * offset, axis=-1, keepdims=True)
    return offset * lax.rsqrt(spread + EPSILON) * gain + shift


def gelu_tanh(values):
    return jax.nn.gelu(values, approximate=True)


def product(left, right):
    return jnp.dot(left, right, preferred_element_type=jnp.float32)


def split_heads(matrix):
    return matrix.reshape(matrix.shape[0], -1, HD)


def on_device(
    inputs,
    cotangent,
    attn_norm_gain,
    attn_norm_bias,
    qkv_weight,
    query_value_bias,
    out_weight,
    out_bias,
    mlp_norm_gain,
    mlp_norm_bias,
    up_weight,
    up_bias,
    down_weight,
    down_bias,
):
    rows_in = inputs[0].astype(jnp.float32)
    upstream = cotangent[0]
    upstream_f = upstream.astype(jnp.float32)
    qkv_full, out_full, up_full, down_full = (
        lax.all_gather(qkv_weight, "shard", axis=1, tiled=True),
        lax.all_gather(out_weight, "shard", axis=1, tiled=True),
        lax.all_gather(up_weight, "shard", axis=0, tiled=True),
        lax.all_gather(down_weight, "shard", axis=1, tiled=True),
    )
    scaling = HD ** (-0.5)
    normed_one, norm_one_back = jax.vjp(layer_norm, rows_in, attn_norm_gain, attn_norm_bias)
    attn_in = normed_one.astype(jnp.bfloat16)
    projected = jnp.einsum("td,cdh->cth", attn_in, qkv_full, preferred_element_type=jnp.float32)
    queries = (projected[0] + query_value_bias[0]).astype(jnp.bfloat16)
    keys_here = projected[1].astype(jnp.bfloat16)
    values_here = (projected[2] + query_value_bias[1]).astype(jnp.bfloat16)
    queries_split = split_heads(queries)
    rows_count = queries.shape[0]
    heads_local = queries_split.shape[1]
    width_local = queries.shape[1]
    run_max = jnp.full((heads_local, rows_count, 1), -jnp.inf, jnp.float32)
    run_total = jnp.zeros((heads_local, rows_count, 1), jnp.float32)
    run_accum = jnp.zeros((heads_local, rows_count, HD), jnp.float32)
    keys_block = lax.all_gather(keys_here, "ctx", axis=0, tiled=True)
    values_block = lax.all_gather(values_here, "ctx", axis=0, tiled=True)
    block_scores = (
        jnp.einsum(
            "qhd,khd->hqk",
            queries_split,
            split_heads(keys_block),
            preferred_element_type=jnp.float32,
        )
        * scaling
    )
    new_max = jnp.max(block_scores, axis=-1, keepdims=True)
    factor = jnp.exp(run_max - new_max)
    block_exp = jnp.exp(block_scores - new_max)
    new_total = run_total * factor + jnp.sum(block_exp, axis=-1, keepdims=True)
    new_accum = run_accum * factor + jnp.einsum(
        "hqk,khd->hqd",
        block_exp.astype(jnp.bfloat16),
        split_heads(values_block),
        preferred_element_type=jnp.float32,
    )
    attended = new_accum / new_total
    log_total = new_max + jnp.log(new_total)
    attended_b = (
        jnp.transpose(attended, (1, 0, 2)).reshape(rows_count, width_local).astype(jnp.bfloat16)
    )
    attn_sum = lax.psum(product(attended_b, out_full).astype(jnp.bfloat16), "tensor").astype(
        jnp.float32
    )
    residual = rows_in + attn_sum + out_bias
    normed_two, norm_two_back = jax.vjp(layer_norm, residual, mlp_norm_gain, mlp_norm_bias)
    mlp_in = normed_two.astype(jnp.bfloat16)
    hidden = product(mlp_in, up_full) + up_bias
    activ_f, gelu_back = jax.vjp(gelu_tanh, hidden)
    activated = activ_f.astype(jnp.bfloat16)
    mlp_sum = lax.psum(product(activated, down_full).astype(jnp.bfloat16), "tensor").astype(
        jnp.float32
    )
    output = (residual + mlp_sum + down_bias).astype(jnp.bfloat16)
    down_bias_grad = jnp.sum(upstream_f, axis=0)
    down_grad = jnp.einsum("tf,td->fd", activated, upstream, preferred_element_type=jnp.float32)
    d_activated = jnp.einsum("td,fd->tf", upstream, down_full, preferred_element_type=jnp.float32)
    (d_hidden,) = gelu_back(d_activated)
    up_bias_grad = jnp.sum(d_hidden, axis=0)
    d_hidden_b = d_hidden.astype(jnp.bfloat16)
    up_grad = jnp.einsum("td,tf->df", mlp_in, d_hidden_b, preferred_element_type=jnp.float32)
    d_mlp_part = jnp.einsum("tf,df->td", d_hidden_b, up_full, preferred_element_type=jnp.float32)
    d_mlp_in = lax.psum(d_mlp_part.astype(jnp.bfloat16), "tensor").astype(jnp.float32)
    d_norm_two, mlp_gain_grad, mlp_shift_grad = norm_two_back(d_mlp_in)
    d_residual = upstream_f + d_norm_two
    out_bias_grad = jnp.sum(d_residual, axis=0)
    d_residual_b = d_residual.astype(jnp.bfloat16)
    out_grad = jnp.einsum("th,td->hd", attended_b, d_residual_b, preferred_element_type=jnp.float32)
    d_attended = jnp.einsum(
        "td,hd->th", d_residual_b, out_full, preferred_element_type=jnp.float32
    ).astype(jnp.bfloat16)
    d_attended_split = split_heads(d_attended)
    delta = jnp.sum(
        d_attended_split.astype(jnp.float32) * split_heads(attended_b).astype(jnp.float32), axis=-1
    )
    delta = jnp.transpose(delta)[:, :, None]
    keys_back, values_back = (
        lax.all_gather(keys_here, "ctx", axis=0, tiled=True),
        lax.all_gather(values_here, "ctx", axis=0, tiled=True),
    )
    keys_split = split_heads(keys_back)
    values_split = split_heads(values_back)
    scores_back = (
        jnp.einsum("qhd,khd->hqk", queries_split, keys_split, preferred_element_type=jnp.float32)
        * scaling
    )
    probs = jnp.exp(scores_back - log_total)
    d_probs = jnp.einsum(
        "qhd,khd->hqk", d_attended_split, values_split, preferred_element_type=jnp.float32
    )
    d_scores_b = (probs * (d_probs - delta)).astype(jnp.bfloat16)
    probs_b = probs.astype(jnp.bfloat16)
    d_queries = (
        jnp.einsum("hqk,khd->qhd", d_scores_b, keys_split, preferred_element_type=jnp.float32)
        * scaling
    ).reshape(rows_count, width_local)
    key_terms = (
        jnp.einsum("hqk,qhd->khd", d_scores_b, queries_split, preferred_element_type=jnp.float32)
        * scaling
    ).reshape(-1, width_local)
    value_terms = jnp.einsum(
        "hqk,qhd->khd", probs_b, d_attended_split, preferred_element_type=jnp.float32
    ).reshape(-1, width_local)
    kv_grad = lax.psum_scatter(
        jnp.concatenate([key_terms, value_terms], axis=1).astype(jnp.bfloat16),
        "ctx",
        scatter_dimension=0,
        tiled=True,
    ).astype(jnp.float32)
    d_keys = kv_grad[:, :width_local]
    d_values = kv_grad[:, width_local:]
    bias_grad = jnp.stack([jnp.sum(d_queries, axis=0), jnp.sum(d_values, axis=0)])
    d_proj = jnp.stack([d_queries, d_keys, d_values]).astype(jnp.bfloat16)
    qkv_grad = jnp.einsum("td,cth->cdh", attn_in, d_proj, preferred_element_type=jnp.float32)
    d_attn_part = jnp.einsum("cth,cdh->td", d_proj, qkv_full, preferred_element_type=jnp.float32)
    d_attn_in = lax.psum(d_attn_part.astype(jnp.bfloat16), "tensor").astype(jnp.float32)
    d_norm_one, attn_gain_grad, attn_shift_grad = norm_one_back(d_attn_in)
    inputs_grad = d_residual + d_norm_one
    matrices = (qkv_grad, out_grad, up_grad, down_grad)
    summed = (
        lax.psum(matrices[0].astype(jnp.bfloat16), "ctx").astype(jnp.float32),
        lax.psum(matrices[1].astype(jnp.bfloat16), "ctx").astype(jnp.float32),
        lax.psum(matrices[2].astype(jnp.bfloat16), "ctx").astype(jnp.float32),
        lax.psum(matrices[3].astype(jnp.bfloat16), "ctx").astype(jnp.float32),
    )
    owned = (
        lax.psum_scatter(
            summed[0].astype(jnp.bfloat16), "shard", scatter_dimension=1, tiled=True
        ).astype(jnp.float32),
        lax.psum_scatter(
            summed[1].astype(jnp.bfloat16), "shard", scatter_dimension=1, tiled=True
        ).astype(jnp.float32),
        lax.psum_scatter(
            summed[2].astype(jnp.bfloat16), "shard", scatter_dimension=0, tiled=True
        ).astype(jnp.float32),
        lax.psum_scatter(
            summed[3].astype(jnp.bfloat16), "shard", scatter_dimension=1, tiled=True
        ).astype(jnp.float32),
    )
    vectors = lax.psum(
        (
            attn_gain_grad,
            attn_shift_grad,
            bias_grad,
            out_bias_grad,
            mlp_gain_grad,
            mlp_shift_grad,
            up_bias_grad,
            down_bias_grad,
        ),
        ("shard", "ctx"),
    )
    return (
        output[None],
        inputs_grad[None],
        vectors[0],
        vectors[1],
        owned[0],
        vectors[2],
        owned[1],
        vectors[3],
        vectors[4],
        vectors[5],
        owned[2],
        vectors[6],
        owned[3],
        vectors[7],
    )


def solution(mesh):
    in_specs = (
        P("shard", "ctx", None),
        P("shard", "ctx", None),
        P(),
        P(),
        P(None, "shard", "tensor"),
        P(None, "tensor"),
        P("tensor", "shard"),
        P(),
        P(),
        P(),
        P("shard", "tensor"),
        P("tensor"),
        P("tensor", "shard"),
        P(),
    )
    out_specs = (
        P("shard", "ctx", None),
        P("shard", "ctx", None),
        P(),
        P(),
        P(None, "shard", "tensor"),
        P(None, "tensor"),
        P("tensor", "shard"),
        P(),
        P(),
        P(),
        P("shard", "tensor"),
        P("tensor"),
        P("tensor", "shard"),
        P(),
    )
    return jax.shard_map(
        on_device, mesh=mesh, in_specs=in_specs, out_specs=out_specs, check_vma=False
    )
```

profile of v0, /device:TPU:0, one launch (start us, length us, event | category | flops | bytes accessed | tf_op | source)
XLA Modules:
  0.0 525.6 jit_solution(9866181186982959166)
XLA Ops:
  12.6 29.7 %all_gather.20 = bf16[3,1152,144]{2,0,1:T(4,128)(2,1)} all-gather(bf16[3,576,144]{2,0,1:T(4,128)(2,1)S(1)} %copy.31), channel_id=1, replica_groups=mesh['shard'=2,'ctx'=2,'tensor'=8] {'shard'}, dimensions={1}, use_global_device_ids=true | all-gather | bytes 1492992 | tf_op jit(solution)/shard_map/all_gather | solution.py:49
  42.3 4.0 copy.32
  52.4 7.3 %all-gather.1 = bf16[2,576,144]{1,2,0:T(8,128)(2,1)S(1)} all-gather(bf16[1,576,144]{1,2,0:T(8,128)(2,1)S(1)} %bitcast.203), channel_id=1, replica_groups=mesh['shard'=2,'ctx'=2,'tensor'=8] {'shard'}, dimensions={0}, use_global_device_ids=true | all-gather | bytes 497664 | tf_op jit(solution)/shard_map/all_gather | solution.py:50
  63.4 3.2 fusion.51
  69.7 80.4 %all-reduce.8.cloned.1.call-done = bf16[512,1152]{1,0:T(8,128)(2,1)} async-done(((bf16[512,1152]{1,0:T(8,128)(2,1)}), bf16[512,1152]{1,0:T(8,128)(2,1)}) %all-reduce.8.cloned.1.call-update) | async-done | bytes 1179664 | tf_op jit(solution)/shard_map/psum | solution.py:94
  152.6 3.5 copy.34
  156.1 4.0 reshape.163
  160.1 3.5 copy.35
  163.6 4.1 reshape.165
  175.9 79.3 %all-reduce.10.cloned.1.call-done = bf16[512,1152]{1,0:T(8,128)(2,1)} async-done(((bf16[512,1152]{1,0:T(8,128)(2,1)}), bf16[512,1152]{1,0:T(8,128)(2,1)}) %all-reduce.10.cloned.1.call-update) | async-done | bytes 1179664 | tf_op jit(solution)/shard_map/psum | solution.py:115
  255.2 2.9 convert_reduce_fusion.1
  272.6 3.7 convolution_convert_fusion
  279.0 3.3 convolution_convert_fusion.1
  290.3 3.3 copy.37
  293.6 5.4 %reshape.170 = bf16[1152,432]{1,0:T(8,128)(2,1)} reshape(bf16[1152,3,144]{2,1,0:T(4,128)(2,1)} %bitcast.178) | data formatting | bytes 1990656
  299.3 4.0 convolution_convert_fusion.4
  307.8 14.7 %reduce-scatter.22.cloned.1.call-done = bf16[576,538]{1,0:T(8,128)(2,1)} async-done(((bf16[1152,538]{1,0:T(8,128)(2,1)}), bf16[576,538]{1,0:T(8,128)(2,1)}) %reduce-scatter.22.cloned.1.call-update) | async-done | bytes 619792
  324.8 24.9 %reduce-scatter.20.cloned.1.call-done = bf16[576,538]{1,0:T(8,128)(2,1)} async-done(((bf16[1152,538]{1,0:T(8,128)(2,1)}), bf16[576,538]{1,0:T(8,128)(2,1)}) %reduce-scatter.20.cloned.1.call-update) | async-done | bytes 619792
  352.0 22.4 %reduce-scatter.16.cloned.1.call-done = bf16[576,432]{1,0:T(8,128)(2,1)} async-done(((bf16[1152,432]{1,0:T(8,128)(2,1)}), bf16[576,432]{1,0:T(8,128)(2,1)}) %reduce-scatter.16.cloned.1.call-update) | async-done | bytes 497680
  374.4 2.9 reshape.171
  379.4 108.3 %all-reduce.12.cloned.1.call-done = (bf16[512,1152]{1,0:T(8,128)(2,1)}, bf16[512,1152]{1,0:T(8,128)(2,1)}) async-done(((bf16[512,1152]{1,0:T(8,128)(2,1)}, bf16[512,1152]{1,0:T(8,128)(2,1)}), (bf16[512,1152]{1,0:T(8,128)(2,1)}, bf16[512,1152]{1,0:T(8,128)(2,1)})) %all-reduce.12.cloned.1.call-update) | async-done | bytes 2359312 | tf_op jit(solution)/shard_map/psum | solution.py:103
  492.3 11.9 %all-reduce = (f32[1152]{0:T(1024)}, f32[1152]{0:T(1024)}, f32[2,144]{1,0:T(2,128)}, f32[1152]{0:T(1024)}, f32[1152]{0:T(1024)}, /*index=5*/f32[1152]{0:T(1024)}, f32[538]{0:T(1024)}, f32[1152]{0:T(1024)}) all-reduce(f32[1152]{0:T(1024)} %get-tuple-element.16, ...), channel_id=1, replica_groups=mesh['shard'=2,'ctx'=2,'tensor'=8] {'shard','ctx'}, use_global_device_ids=true, to_apply=%region_17.0 | all-reduce | flops 7738 | bytes 61904 | tf_op jit(solution)/shard_map/psum | solution.py:192
  504.8 4.2 add_bitcast_fusion
  509.0 3.1 all-reduce.14.cloned.1.call-done
  (172 shorter events, 75.7 us)
Async XLA Ops:
  8.0 142.1 %all-reduce.8.cloned.1.call-start = ((), (), s32[]{:S(2)}) async-start(), calls=%async_computation.5 | async-start | bytes 2359296 | tf_op jit(solution)/shard_map/psum | solution.py:94
  9.6 279.0 %copy-start.29 = (f32[512]{0:T(512)}, f32[512]{0:T(512)S(1)}, u32[]{:S(2)}) copy-start(f32[512]{0:T(512)S(1)} %broadcast_multiply_fusion.1) | copy-start | bytes 6148
  11.4 277.3 %copy-start.34 = (f32[512]{0:T(512)}, f32[512]{0:T(512)S(1)}, u32[]{:S(2)}) copy-start(f32[512]{0:T(512)S(1)} %fusion.70) | copy-start | bytes 6148
  42.3 4.0 copy-start.28
  42.3 4.0 copy-start.38
  51.3 8.5 %copy-start.1 = (f32[2,512,1024]{2,1,0:T(8,128)}, f32[2,512,1024]{2,1,0:T(8,128)S(1)}, u32[]{:S(2)}) copy-start(f32[2,512,1024]{2,1,0:T(8,128)S(1)} %get-tuple-element.50) | copy-start | bytes 12582916
  66.6 83.4 %copy-start.21 = (f32[1152]{0:T(1024)S(1)}, f32[1152]{0:T(1024)}, u32[]{:S(2)}) copy-start(f32[1152]{0:T(1024)} %param.21) | copy-start | bytes 13828
  68.3 84.3 %all-gather.7.cloned.1.call-start = ((), (), s32[]{:S(2)}) async-start(), calls=%async_computation.8 | async-start | bytes 2088960 | tf_op jit(solution)/shard_map/all_gather | solution.py:51
  68.8 91.3 %all-gather.9.cloned.1.call-start = ((), (), s32[]{:S(2)}) async-start(), calls=%async_computation.9 | async-start | bytes 2088960 | tf_op jit(solution)/shard_map/all_gather | solution.py:52
  69.4 185.8 %all-reduce.10.cloned.1.call-start = ((), (), s32[]{:S(2)}) async-start(), calls=%async_computation.6 | async-start | bytes 2359296 | tf_op jit(solution)/shard_map/psum | solution.py:115
  160.1 7.6 %copy-start.27 = (f32[1152]{0:T(1024)S(1)}, f32[1152]{0:T(1024)}, u32[]{:S(2)}) copy-start(f32[1152]{0:T(1024)} %param.22) | copy-start | bytes 13828
  160.1 7.6 %copy-start.37 = (f32[1152]{0:T(1024)S(1)}, f32[1152]{0:T(1024)}, u32[]{:S(2)}) copy-start(f32[1152]{0:T(1024)} %param.23) | copy-start | bytes 13828
  160.1 7.6 %copy-start.40 = (f32[538]{0:T(1024)S(1)}, f32[538]{0:T(1024)}, u32[]{:S(2)}) copy-start(f32[538]{0:T(1024)} %param.25) | copy-start | bytes 6460
  175.6 112.0 %reduce-scatter.14.cloned.1.call-start = ((), (), s32[]{:S(2)}) async-start(), calls=%async_computation.7 | async-start | bytes 884736 | tf_op jit(solution)/shard_map/reduce_scatter | solution.py:156
  260.1 4.2 copy-start.2
  269.4 36.0 %reduce-scatter.18.cloned.1.call-start = ((), (), s32[]{:S(2)}) async-start(), calls=%async_computation.11 | async-start | bytes 884736
  272.6 49.9 %reduce-scatter.22.cloned.1.call-start = ((), (), s32[]{:S(2)}) async-start(), calls=%async_computation.13 | async-start | bytes 2211840
  279.0 70.7 %reduce-scatter.20.cloned.1.call-start = ((), (), s32[]{:S(2)}) async-start(), calls=%async_computation.12 | async-start | bytes 2211840
  284.8 4.5 copy-start.39
  284.9 89.5 %reduce-scatter.16.cloned.1.call-start = ((), (), s32[]{:S(2)}) async-start(), calls=%async_computation.10 | async-start | bytes 1769472
  299.0 4.3 copy-start.15
  299.0 188.7 %all-reduce.12.cloned.1.call-start = ((), (), s32[]{:S(2)}) async-start(), calls=%async_computation.14 | async-start | bytes 4718592 | tf_op jit(solution)/shard_map/psum | solution.py:103
  305.2 207.0 %all-reduce.14.cloned.1.call-start = ((), (), s32[]{:S(2)}) async-start(), calls=%async_computation.15 | async-start | bytes 4259840 | tf_op jit(solution)/shard_map/psum | solution.py:173
  512.2 5.1 copy-start.16
  (30 other events, 66.5 us)
Sparse Core Ops, SparseCore 0:
  68.4 81.6 all-reduce.7
  175.7 79.4 all-reduce.9
  269.5 7.1 reduce-scatter.13
  278.8 16.4 reduce-scatter.17
  297.4 25.0 reduce-scatter.21
  324.6 25.0 reduce-scatter.19
  352.5 21.8 reduce-scatter.15
  379.1 108.5 all-reduce.11
  491.4 20.6 all-reduce.13
Sparse Core Ops, SparseCore 1:
  70.3 26.5 all-gather.6
  98.3 25.0 all-gather.8
where the time goes:
time: 527 us; the launch traced here: 526 us
  waiting for transfers between devices  334 us (63%)
  local copies, waits for them, and re-layouts  53.7 us (10%)
  blocking collectives  52.9 us (10%)
  matrix products  35.4 us (7%)
  other arithmetic  32.1 us (6%)
  between operations  15.8 us (3%)
    psum x1, waiting for transfers between devices, on_device(): lax.psum(product(activated, down_full).astype(jnp.bfloat16), 'tensor')  108 us
    psum x1, waiting for transfers between devices, on_device(): lax.psum(product(attended_b, out_full).astype(jnp.bfloat16), 'tensor')  80.4 us
    psum x1, waiting for transfers between devices, on_device(): lax.psum(d_mlp_part.astype(jnp.bfloat16), 'tensor').astype(jnp.float32)  79.3 us
    unnamed x15, waiting for transfers between devices  63.2 us
    unnamed x100, local copies, waits for them, and re-layouts  41.2 us
    all_gather x1, blocking collectives, on_device(): lax.all_gather(qkv_weight, 'shard', axis=1, tiled=True)  29.7 us
    psum x1, blocking collectives, on_device(): lax.psum((attn_gain_grad, attn_shift_grad, bias_grad, out_bias_grad, mlp_...  11.9 us
  transfers between devices with their start and end apart: 11, of which 7 were waited for; matrix products, arithmetic and copies ran while one was open for 13% of the time, Pallas kernels for 0%

commit v1 on v0

--- a/solution.py
+++ b/solution.py
@@ -5,6 +5,27 @@
 
 HD = 72
 EPSILON = 1e-06
+
+
+def joined_along(parts, dim):
+    lengths = list(parts.shape[1:])
+    lengths[dim] *= parts.shape[0]
+    return jnp.moveaxis(parts, 0, dim).reshape(lengths)
+
+
+def collected_by_bits(x, axis):
+    devices, index = (lax.axis_size(axis), lax.axis_index(axis))
+    parts, bit = (x[None], 1)
+    while bit < devices:
+        other = lax.ppermute(parts, axis, [(i, i ^ bit) for i in range(devices)])
+        low = index & bit == 0
+        parts = jnp.concatenate([jnp.where(low, parts, other), jnp.where(low, other, parts)])
+        bit *= 2
+    return parts
+
+
+def collect(x, axis, dim):
+    return joined_along(collected_by_bits(x, axis), dim)
 
 
 def layer_norm(rows, gain, shift):
@@ -46,7 +67,7 @@
     upstream = cotangent[0]
     upstream_f = upstream.astype(jnp.float32)
     qkv_full, out_full, up_full, down_full = (
-        lax.all_gather(qkv_weight, "shard", axis=1, tiled=True),
+        collect(qkv_weight, "shard", 1),
         lax.all_gather(out_weight, "shard", axis=1, tiled=True),
         lax.all_gather(up_weight, "shard", axis=0, tiled=True),
         lax.all_gather(down_weight, "shard", axis=1, tiled=True),

time: 527 us -> 497 us (0.943); the launches traced: 526 us -> 490 us
  waiting for transfers between devices: 334 us -> 319 us
  blocking collectives: 52.9 us -> 38 us
    all_gather x1 -> x0, blocking collectives: 29.7 us -> none  [on_device(): lax.all_gather(qkv_weight, 'shard', axis=1, tiled=True)]
    psum x1, waiting for transfers between devices: 80.4 us -> 51.8 us  [on_device(): lax.psum(product(attended_b, out_full).astype(jnp.bfloat16), 'tensor')]
    all_gather x1, blocking collectives: 7.34 us -> 22.1 us  [on_device(): lax.all_gather(out_weight, 'shard', axis=1, tiled=True)]
    all_gather x1, waiting for transfers between devices: 0.02 us -> 14.5 us  [on_device(): lax.all_gather(down_weight, 'shard', axis=1, tiled=True)]
    unnamed x100 -> x99, local copies, waits for them, and re-layouts: 41.2 us -> 40.3 us
  transfers between devices with their start and end apart: 11 -> 12, of which waited for: 7 -> 8; matrix products, arithmetic and copies ran while one was open for 13% -> 17% of each run, Pallas kernels for 0% -> 0%
where the time goes in v1:
time: 497 us; the launch traced here: 490 us
  waiting for transfers between devices  319 us (64%)
  local copies, waits for them, and re-layouts  50.4 us (10%)
  blocking collectives  38 us (8%)
  matrix products  31.7 us (6%)
  other arithmetic  30.2 us (6%)
  between operations  16.6 us (3%)
    psum x1, waiting for transfers between devices, on_device(): lax.psum(product(activated, down_full).astype(jnp.bfloat16), 'tensor')  108 us
    psum x1, waiting for transfers between devices, on_device(): lax.psum(d_mlp_part.astype(jnp.bfloat16), 'tensor').astype(jnp.float32)  78.8 us
    unnamed x15, waiting for transfers between devices  62.9 us
    psum x1, waiting for transfers between devices, on_device(): lax.psum(product(attended_b, out_full).astype(jnp.bfloat16), 'tensor')  51.8 us
    unnamed x99, local copies, waits for them, and re-layouts  40.3 us
    all_gather x1, blocking collectives, on_device(): lax.all_gather(out_weight, 'shard', axis=1, tiled=True)  22.1 us
    all_gather x1, waiting for transfers between devices, on_device(): lax.all_gather(down_weight, 'shard', axis=1, tiled=True)  14.5 us
    psum x1, blocking collectives, on_device(): lax.psum((attn_gain_grad, attn_shift_grad, bias_grad, out_bias_grad, mlp_...  11.9 us
  transfers between devices with their start and end apart: 12, of which 8 were waited for; matrix products, arithmetic and copies ran while one was open for 17% of the time, Pallas kernels for 0%

profile of v1, /device:TPU:0, one launch (start us, length us, event | category | flops | bytes accessed | tf_op | source)
XLA Modules:
  0.0 490.0 jit_solution(12188898102924258061)
XLA Ops:
  8.8 3.0 collective-permute-start
  13.6 22.1 %all-gather.1 = bf16[2,576,144]{1,2,0:T(8,128)(2,1)S(1)} all-gather(bf16[1,576,144]{1,2,0:T(8,128)(2,1)S(1)} %bitcast.206), channel_id=1, replica_groups=mesh['shard'=2,'ctx'=2,'tensor'=8] {'shard'}, dimensions={0}, use_global_device_ids=true | all-gather | bytes 497664 | tf_op jit(solution)/shard_map/all_gather | solution.py:71
  49.8 3.5 copy.35
  53.3 4.1 reshape.194
  57.4 14.5 %all-gather.9.cloned.1.call-done = bf16[2,576,538]{1,2,0:T(8,128)(2,1)} async-done(((bf16[1,576,538]{1,2,0:T(8,128)(2,1)}), bf16[2,576,538]{1,2,0:T(8,128)(2,1)}) %all-gather.9.cloned.1.call-update) | async-done | bytes 1239568 | tf_op jit(solution)/shard_map/all_gather | solution.py:73
  72.0 3.5 copy.36
  75.4 4.1 reshape.196
  79.5 51.8 %all-reduce.8.cloned.1.call-done = bf16[512,1152]{1,0:T(8,128)(2,1)} async-done(((bf16[512,1152]{1,0:T(8,128)(2,1)}), bf16[512,1152]{1,0:T(8,128)(2,1)}) %all-reduce.8.cloned.1.call-update) | async-done | bytes 1179664 | tf_op jit(solution)/shard_map/psum | solution.py:115
  141.0 78.8 %all-reduce.10.cloned.1.call-done = bf16[512,1152]{1,0:T(8,128)(2,1)} async-done(((bf16[512,1152]{1,0:T(8,128)(2,1)}), bf16[512,1152]{1,0:T(8,128)(2,1)}) %all-reduce.10.cloned.1.call-update) | async-done | bytes 1179664 | tf_op jit(solution)/shard_map/psum | solution.py:136
  219.8 2.9 convert_reduce_fusion.1
  237.3 3.7 convolution_convert_fusion
  243.6 3.3 convolution_convert_fusion.1
  254.9 3.3 copy.37
  258.2 5.4 %reshape.200 = bf16[1152,432]{1,0:T(8,128)(2,1)} reshape(bf16[1152,3,144]{2,1,0:T(4,128)(2,1)} %bitcast.184) | data formatting | bytes 1990656
  263.9 4.0 convolution_convert_fusion.4
  272.4 14.8 %reduce-scatter.22.cloned.1.call-done = bf16[576,538]{1,0:T(8,128)(2,1)} async-done(((bf16[1152,538]{1,0:T(8,128)(2,1)}), bf16[576,538]{1,0:T(8,128)(2,1)}) %reduce-scatter.22.cloned.1.call-update) | async-done | bytes 619792
  289.5 25.0 %reduce-scatter.20.cloned.1.call-done = bf16[576,538]{1,0:T(8,128)(2,1)} async-done(((bf16[1152,538]{1,0:T(8,128)(2,1)}), bf16[576,538]{1,0:T(8,128)(2,1)}) %reduce-scatter.20.cloned.1.call-update) | async-done | bytes 619792
  316.8 22.2 %reduce-scatter.16.cloned.1.call-done = bf16[576,432]{1,0:T(8,128)(2,1)} async-done(((bf16[1152,432]{1,0:T(8,128)(2,1)}), bf16[576,432]{1,0:T(8,128)(2,1)}) %reduce-scatter.16.cloned.1.call-update) | async-done | bytes 497680
  339.0 2.9 reshape.201
  344.0 107.8 %all-reduce.12.cloned.1.call-done = (bf16[512,1152]{1,0:T(8,128)(2,1)}, bf16[512,1152]{1,0:T(8,128)(2,1)}) async-done(((bf16[512,1152]{1,0:T(8,128)(2,1)}, bf16[512,1152]{1,0:T(8,128)(2,1)}), (bf16[512,1152]{1,0:T(8,128)(2,1)}, bf16[512,1152]{1,0:T(8,128)(2,1)})) %all-reduce.12.cloned.1.call-update) | async-done | bytes 2359312 | tf_op jit(solution)/shard_map/psum | solution.py:124
  451.9 2.7 convert_reduce_fusion
  456.4 11.9 %all-reduce = (f32[1152]{0:T(1024)}, f32[1152]{0:T(1024)}, f32[2,144]{1,0:T(2,128)}, f32[1152]{0:T(1024)}, f32[1152]{0:T(1024)}, /*index=5*/f32[1152]{0:T(1024)}, f32[538]{0:T(1024)}, f32[1152]{0:T(1024)}) all-reduce(f32[1152]{0:T(1024)} %get-tuple-element.16, ...), channel_id=1, replica_groups=mesh['shard'=2,'ctx'=2,'tensor'=8] {'shard','ctx'}, use_global_device_ids=true, to_apply=%region_17.18 | all-reduce | flops 7738 | bytes 61904 | tf_op jit(solution)/shard_map/psum | solution.py:213
  469.0 4.2 add_bitcast_fusion
  473.2 2.7 all-reduce.14.cloned.1.call-done
  (175 shorter events, 71.2 us)
Async XLA Ops:
  8.0 29.0 %copy-start = (bf16[1,512,1152]{2,1,0:T(8,128)(2,1)S(1)}, bf16[1,512,1152]{2,1,0:T(8,128)(2,1)}, u32[]{:S(2)}) copy-start(bf16[1,512,1152]{2,1,0:T(8,128)(2,1)} %param.14) | copy-start | bytes 3538948
  8.0 5.5 %copy-start.36 = (f32[2,144]{1,0:T(2,128)S(1)}, f32[2,144]{1,0:T(2,128)}, u32[]{:S(2)}) copy-start(f32[2,144]{1,0:T(2,128)} %param.19) | copy-start | bytes 3460
  8.0 5.6 %copy-start.22 = (bf16[144,576]{1,0:T(8,128)(2,1)S(1)}, bf16[144,576]{1,0:T(8,128)(2,1)}, u32[]{:S(2)}) copy-start(bf16[144,576]{1,0:T(8,128)(2,1)} %param.20) | copy-start | bytes 497668
  8.0 41.8 %all-gather.7.cloned.1.call-start = ((), (), s32[]{:S(2)}) async-start(), calls=%async_computation.8 | async-start | bytes 2088960 | tf_op jit(solution)/shard_map/all_gather | solution.py:72
  8.8 63.2 %all-gather.9.cloned.1.call-start = ((), (), s32[]{:S(2)}) async-start(), calls=%async_computation.9 | async-start | bytes 2088960 | tf_op jit(solution)/shard_map/all_gather | solution.py:73
  8.8 28.7 %collective-permute-start = (bf16[1,3,576,144]{2,3,1,0:T(8,128)(2,1)}, bf16[1,3,576,144]{2,3,1,0:T(8,128)(2,1)S(1)}, u32[]{:S(2)}, u32[]{:S(2)}) collective-permute-start(bf16[1,3,576,144]{2,3,1,0:T(8,128)(2,1)} %bitcast.204), channel_id=1, source_target_pairs={{0,16},{16,0},{1,17},{17,1},{2,18},{18,2},{3,19},{19,3},{4,20},{20... | collective-permute-start | bytes 1493000 | tf_op jit(solution)/shard_map/ppermute | solution.py:20
  11.9 25.6 %copy-start.20 = (bf16[3,576,144]{1,2,0:T(8,128)(2,1)S(1)}, bf16[3,576,144]{1,2,0:T(8,128)(2,1)}, u32[]{:S(2)}) copy-start(bf16[3,576,144]{1,2,0:T(8,128)(2,1)} %param.18) | copy-start | bytes 1492996
  11.9 119.4 %all-reduce.8.cloned.1.call-start = ((), (), s32[]{:S(2)}) async-start(), calls=%async_computation.5 | async-start | bytes 2359296 | tf_op jit(solution)/shard_map/psum | solution.py:115
  13.5 239.8 %copy-start.29 = (f32[512]{0:T(512)}, f32[512]{0:T(512)S(1)}, u32[]{:S(2)}) copy-start(f32[512]{0:T(512)S(1)} %broadcast_multiply_fusion.1) | copy-start | bytes 6148
  37.5 215.8 %copy-start.34 = (f32[512]{0:T(512)}, f32[512]{0:T(512)S(1)}, u32[]{:S(2)}) copy-start(f32[512]{0:T(512)S(1)} %fusion.85) | copy-start | bytes 6148
  49.3 170.6 %all-reduce.10.cloned.1.call-start = ((), (), s32[]{:S(2)}) async-start(), calls=%async_computation.6 | async-start | bytes 2359296 | tf_op jit(solution)/shard_map/psum | solution.py:136
  57.4 73.9 %copy-start.21 = (f32[1152]{0:T(1024)S(1)}, f32[1152]{0:T(1024)}, u32[]{:S(2)}) copy-start(f32[1152]{0:T(1024)} %param.21) | copy-start | bytes 13828
  79.5 54.3 %copy-start.27 = (f32[1152]{0:T(1024)S(1)}, f32[1152]{0:T(1024)}, u32[]{:S(2)}) copy-start(f32[1152]{0:T(1024)} %param.22) | copy-start | bytes 13828
  79.5 54.4 %copy-start.37 = (f32[1152]{0:T(1024)S(1)}, f32[1152]{0:T(1024)}, u32[]{:S(2)}) copy-start(f32[1152]{0:T(1024)} %param.23) | copy-start | bytes 13828
  79.5 54.4 %copy-start.40 = (f32[538]{0:T(1024)S(1)}, f32[538]{0:T(1024)}, u32[]{:S(2)}) copy-start(f32[538]{0:T(1024)} %param.25) | copy-start | bytes 6460
  140.8 111.4 %reduce-scatter.14.cloned.1.call-start = ((), (), s32[]{:S(2)}) async-start(), calls=%async_computation.7 | async-start | bytes 884736 | tf_op jit(solution)/shard_map/reduce_scatter | solution.py:177
  234.0 35.9 %reduce-scatter.18.cloned.1.call-start = ((), (), s32[]{:S(2)}) async-start(), calls=%async_computation.11 | async-start | bytes 884736
  237.2 50.0 %reduce-scatter.22.cloned.1.call-start = ((), (), s32[]{:S(2)}) async-start(), calls=%async_computation.13 | async-start | bytes 2211840
  243.6 70.9 %reduce-scatter.20.cloned.1.call-start = ((), (), s32[]{:S(2)}) async-start(), calls=%async_computation.12 | async-start | bytes 2211840
  249.5 4.5 copy-start.39
  249.5 89.5 %reduce-scatter.16.cloned.1.call-start = ((), (), s32[]{:S(2)}) async-start(), calls=%async_computation.10 | async-start | bytes 1769472
  263.6 188.3 %all-reduce.12.cloned.1.call-start = ((), (), s32[]{:S(2)}) async-start(), calls=%async_computation.14 | async-start | bytes 4718592 | tf_op jit(solution)/shard_map/psum | solution.py:124
  269.8 206.1 %all-reduce.14.cloned.1.call-start = ((), (), s32[]{:S(2)}) async-start(), calls=%async_computation.15 | async-start | bytes 4259840 | tf_op jit(solution)/shard_map/psum | solution.py:194
  475.9 5.1 %copy-start.17 = (bf16[538,576]{1,0:T(8,128)(2,1)S(1)}, bf16[538,576]{1,0:T(8,128)(2,1)}, u32[]{:S(2)}) copy-start(bf16[538,576]{1,0:T(8,128)(2,1)} %get-tuple-element.35) | copy-start | bytes 1859332
  (31 other events, 66.2 us)
Sparse Core Ops, SparseCore 0:
  10.4 33.2 all-gather.6
  45.3 26.6 all-gather.8
Sparse Core Ops, SparseCore 1:
  49.4 81.9 all-reduce.7
  140.9 78.9 all-reduce.9
  234.1 7.1 reduce-scatter.13
  243.5 16.3 reduce-scatter.17
  262.2 25.0 reduce-scatter.21
  289.5 25.0 reduce-scatter.19
  317.2 21.7 reduce-scatter.15
  343.6 108.2 all-reduce.11
  455.4 20.4 all-reduce.13
